TPU v7x, 256 devices: a whole 4x4x8 slice. The times are simulated.
256 devices in a mesh: tok: 32 (over z, y_hi, core), row: 2 (over y_lo), col: 4 (over x).
Axes of the slice: x: 4, y: 4 (y_hi: 2, y_lo: 2; y = y_hi * 2 + y_lo), z: 8, core: 2. Of those that a mesh axis runs over, the one named last changes fastest.
Arguments:
- activations: bfloat16 [11264, 4096], P(('tok', 'row'), 'col'), may hold values from -512 to 512
- norm_gain: bfloat16 [4096], P('col'), may hold values from 1.5 to 10
- qkv_weight: bfloat16 [4096, 16, 384], P('row', 'col'), may hold values from -0.09375 to 0.09375
- doc_ids: int32 [11264], P(('tok', 'row')), may hold values from 0 to 3, never falling along the last dimension, each value on 1 to 8448 neighbouring positions
Outputs:
- attended: bfloat16 [11264, 2048], P(('tok', 'row'), 'col')
Inputs may be any that keep to these rules, and one draw needn't show every extreme that they name: `doc_ids`: never falls along the sequence; each of the 4 documents holds 1 to 8448 tokens and one holds exactly 8448.
All inputs are finite; a program needn't handle non-finite values.
Results may differ from a plain program's by a relative error of at most 0.007.
The roundings to bfloat16 on the way count: a program that leaves them out, or rounds other values in their place, can miss the bound.
Values may be sent and summed in bfloat16 or wider, within the bound.
A program may use at most 128 MiB of HBM per device.

v0:
```python
import math

import jax
import jax.numpy as jnp
from jax import lax
from jax.sharding import PartitionSpec as P


def rotate(vectors, places):
    half = vectors.shape[-1] // 2
    spacing = jnp.arange(half).astype(jnp.float32) * (2.0 / vectors.shape[-1])
    inverse = jnp.power(10000.0, -spacing)
    angles = places.astype(jnp.float32)[:, None] * inverse[None, :]
    cosine = jnp.cos(angles)[:, None, :]
    sine = jnp.sin(angles)[:, None, :]
    first_half = vectors[..., :half]
    second_half = vectors[..., half:]
    return jnp.concatenate(
        [first_half * cosine - second_half * sine, first_half * sine + second_half * cosine],
        axis=-1,
    )


def per_device(activations, norm_gain, qkv_weight, doc_ids):
    row_count = activations.shape[0]
    whole, gain_whole = (
        lax.all_gather(activations, "col", axis=1, tiled=True),
        lax.all_gather(norm_gain, "col", axis=0, tiled=True),
    )
    widened = whole.astype(jnp.float32)
    mean_square = jnp.mean(widened * widened, axis=1, keepdims=True)
    normed = (widened * lax.rsqrt(mean_square + 1e-05) * gain_whole.astype(jnp.float32)).astype(
        jnp.bfloat16
    )
    span, local_heads, width = qkv_weight.shape
    head_size = width // 3
    flat_weight = qkv_weight.reshape(span, local_heads * width)
    projected = jnp.dot(
        normed,
        lax.all_gather(flat_weight, "row", axis=0, tiled=True),
        preferred_element_type=jnp.float32,
    )
    projected = projected.reshape(row_count, local_heads, width)
    first = (lax.axis_index("tok") * lax.axis_size("row") + lax.axis_index("row")) * row_count
    places = first + jnp.arange(row_count, dtype=jnp.int32)
    query = rotate(projected[..., :head_size], places).astype(jnp.bfloat16)
    keys = rotate(projected[..., head_size : 2 * head_size], places).astype(jnp.bfloat16)
    values = projected[..., 2 * head_size :].astype(jnp.bfloat16)
    scale = 1.0 / math.sqrt(head_size)

    def update(state, block_keys, block_values, block_docs, key_places):
        running, totals, summed = state
        scores = (
            jnp.einsum("qhd,khd->hqk", query, block_keys, preferred_element_type=jnp.float32)
            * scale
        )
        visible = (key_places[None, None, :] <= places[None, :, None]) & (
            block_docs[None, None, :] == doc_ids[None, :, None]
        )
        masked = jnp.where(visible, scores, -jnp.inf)
        newest = jnp.maximum(running, jnp.max(masked, axis=2))
        factor = jnp.exp(running - newest)
        exponentials = jnp.where(visible, jnp.exp(masked - newest[:, :, None]), 0.0)
        weights = exponentials.astype(jnp.bfloat16)
        totals = totals * factor + jnp.sum(exponentials, axis=2)
        summed = summed * factor.T[:, :, None] + jnp.einsum(
            "hqk,khd->qhd", weights, block_values, preferred_element_type=jnp.float32
        )
        return (newest, totals, summed)

    initial = (
        jnp.full((local_heads, row_count), -1e30, jnp.float32),
        jnp.zeros((local_heads, row_count), jnp.float32),
        jnp.zeros((row_count, local_heads, head_size), jnp.float32),
    )
    pair_keys, pair_values, pair_docs = (
        lax.all_gather(keys, "row", axis=0, tiled=True),
        lax.all_gather(values, "row", axis=0, tiled=True),
        lax.all_gather(doc_ids, "row", axis=0, tiled=True),
    )
    state = initial
    block_keys = lax.all_gather(pair_keys, "tok", axis=0, tiled=True)
    block_values = lax.all_gather(pair_values, "tok", axis=0, tiled=True)
    block_docs = lax.all_gather(pair_docs, "tok", axis=0, tiled=True)
    count = block_keys.shape[0]
    key_places = jnp.arange(count, dtype=jnp.int32)
    rounds = count // 1024
    stacked = (
        block_keys.reshape(rounds, 1024, local_heads, head_size),
        block_values.reshape(rounds, 1024, local_heads, head_size),
        block_docs.reshape(rounds, 1024),
        key_places.reshape(rounds, 1024),
    )

    def advance(carried, blocks):
        return (update(carried, blocks[0], blocks[1], blocks[2], blocks[3]), None)

    state, unused = lax.scan(advance, state, stacked)
    running, totals, summed = state
    attended = summed / totals.T[:, :, None]
    return attended.reshape(row_count, local_heads * head_size).astype(jnp.bfloat16)


def solution(mesh):
    placed = (P(("tok", "row"), "col"), P("col"), P("row", "col", None), P(("tok", "row")))
    return jax.shard_map(
        per_device, mesh=mesh, in_specs=placed, out_specs=P(("tok", "row"), "col"), check_vma=False
    )
```

profile of v0, /device:TPU:1, one launch (start us, length us, event | category | flops | bytes accessed | tf_op | source)
XLA Modules:
  0.0 528.5 jit_solution(10905290454342149251)
XLA Ops:
  7.3 6.6 %copy.35 = bf16[256,8,4,384]{3,1,2,0:T(8,128)(2,1)} copy(bf16[256,8,4,384]{3,2,1,0:T(4,128)(2,1)} %bitcast.72) | data formatting | bytes 12582912
  14.5 9.3 %all_gather.30 = bf16[4096]{0:T(1024)(128)(2,1)S(1)} all-gather(bf16[1024]{0:T(1024)(128)(2,1)S(1)} %copy-done.1), channel_id=1, replica_groups=mesh['tok'=32,'row'=2,'col'=4] {'col'}, dimensions={0}, use_global_device_ids=true | all-gather | bytes 10240 | tf_op jit(solution)/shard_map/all_gather | solution.py:28
  24.3 16.4 %all-gather.5.cloned.1.call-done = bf16[176,4096]{1,0:T(8,128)(2,1)} async-done(((bf16[176,1024]{1,0:T(8,128)(2,1)}), bf16[176,4096]{1,0:T(8,128)(2,1)}) %all-gather.5.cloned.1.call-update) | async-done | bytes 1441808 | tf_op jit(solution)/shard_map/all_gather | solution.py:27
  42.4 158.1 %all-gather.7.cloned.1.call-done = bf16[4096,1536]{1,0:T(8,128)(2,1)} async-done(((bf16[2048,1536]{1,0:T(8,128)(2,1)}), bf16[4096,1536]{1,0:T(8,128)(2,1)}) %all-gather.7.cloned.1.call-update) | async-done | bytes 12582928 | tf_op jit(solution)/shard_map/all_gather | solution.py:40
  200.5 7.5 %fusion.29 = f32[176,1536]{1,0:T(8,128)S(1)} fusion(bf16[4096,1536]{1,0:T(8,128)(2,1)} %all-gather.7.cloned.1.call-done, bf16[176,4096]{1,0:T(8,128)(2,1)} %all-gather.5.cloned.1.call-done, f32[4096]{0:T(1024)S(1)} %convert_element_type.38, f32[176]{0:T(256)S(1)} %add_rsqrt_fusion), kind=kOutput, calls=%fused_computation.35 | convolution fusion | flops 2217476096 | bytes 15123136 | tf_op jit(solution)/shard_map/dot_general | solution.py:38
  209.3 6.0 %all_gather.32 = bf16[352,4,128]{2,0,1:T(8,128)(2,1)} all-gather(bf16[176,4,128]{2,0,1:T(8,128)(2,1)S(1)} %pad_maximum_fusion), channel_id=1, replica_groups=mesh['tok'=32,'row'=2,'col'=4] {'row'}, dimensions={0}, use_global_device_ids=true | all-gather | bytes 540672 | tf_op jit(solution)/shard_map/all_gather | solution.py:77
  215.5 5.1 all_gather.34
  223.3 3.1 all-reduce
  226.7 129.4 %all-reduce.1 = s32[11264]{0:T(1024)S(1)} all-reduce(s32[11264]{0:T(1024)S(1)} %dynamic-update-slice.1), channel_id=1, replica_groups=mesh['tok'=32,'row'=2,'col'=4] {'tok'}, use_global_device_ids=true, to_apply=%add.1 | all-reduce | flops 11264 | bytes 90112
  356.9 86.2 %all-gather.11.cloned.1.call-done = bf16[11264,4,128]{2,0,1:T(8,128)(2,1)} async-done(((bf16[352,4,128]{2,0,1:T(8,128)(2,1)}), bf16[11264,4,128]{2,0,1:T(8,128)(2,1)}) %all-gather.11.cloned.1.call-update) | async-done | bytes 11534352 | tf_op jit(solution)/shard_map/all_gather | solution.py:83
  443.1 77.1 %while.15 = (s32[]{:T(128)}, f32[4,176]{1,0:T(4,128)S(1)}, f32[4,176]{1,0:T(4,128)S(1)}, f32[176,4,128]{2,0,1:T(8,128)}, s32[11,1024]{1,0:T(8,128)}, /*index=5*/...) while((s32[]{:T(128)}, f32[4,176]{1,0:T(4,128)S(1)}, ...), condition=%wide.region_4.5_spmd.clone, body=%wide.region_1.4_spmd.clone.sunk | while | flops 379285824 | bytes 12442833 | solution.py:98
  446.1 2.9 fusion.53
  453.0 3.0 fusion.53
  458.0 2.0 fusion.49
  460.0 3.0 fusion.53
  467.0 3.0 fusion.53
  472.1 2.0 fusion.49
  474.1 3.0 fusion.53
  481.1 3.0 fusion.53
  488.1 3.0 fusion.53
  495.1 3.0 fusion.53
  502.1 3.0 fusion.53
  509.1 3.0 fusion.53
  516.1 3.0 fusion.53
  (128 shorter events, 48.8 us)
Async XLA Ops:
  6.5 34.2 %all-gather.5.cloned.1.call-start = ((), (), s32[]{:S(2)}) async-start(), calls=%async_computation | async-start | bytes 1802240 | tf_op jit(solution)/shard_map/all_gather | solution.py:27
  7.3 193.3 %all-gather.7.cloned.1.call-start = ((), (), s32[]{:S(2)}) async-start(), calls=%async_computation.1 | async-start | bytes 18874368 | tf_op jit(solution)/shard_map/all_gather | solution.py:40
  13.9 0.7 copy-start.1
  13.9 343.0 %all-gather.9.cloned.1.call-start = ((), (), s32[]{:S(2)}) async-start(), calls=%async_computation.2 | async-start | bytes 11894784 | tf_op jit(solution)/shard_map/all_gather | solution.py:82
  208.9 11.8 %copy-start.3 = (u32[256]{0:T(256)S(1)}, u32[256]{0:T(256)}, u32[]{:S(2)}) copy-start(u32[256]{0:T(256)} %constant.56) | copy-start | bytes 3076
  208.9 12.4 %copy-start.2 = (u32[256]{0:T(256)S(1)}, u32[256]{0:T(256)}, u32[]{:S(2)}) copy-start(u32[256]{0:T(256)} %constant.61) | copy-start | bytes 3076
  208.9 14.1 %copy-start = (s32[176]{0:T(256)S(1)}, s32[176]{0:T(256)}, u32[]{:S(2)}) copy-start(s32[176]{0:T(256)} %param.9) | copy-start | bytes 2116
  215.3 227.8 %all-gather.11.cloned.1.call-start = ((), (), s32[]{:S(2)}) async-start(), calls=%async_computation.3 | async-start | bytes 11894784 | tf_op jit(solution)/shard_map/all_gather | solution.py:83
Sparse Core Ops, SparseCore 0:
  9.1 31.5 all-gather.4
  42.5 157.9 all-gather.6
  215.4 115.8 all-gather.8
  334.0 109.0 all-gather.10
where the time goes:
time: 530 us; the launch traced here: 529 us
  waiting for transfers between devices  262 us (49%)
  blocking collectives  153 us (29%)
  matrix products  62.1 us (12%)
  other arithmetic  18.5 us (3%)
  local copies, waits for them, and re-layouts  18.3 us (3%)
  between operations  14.5 us (3%)
    all_gather x1, waiting for transfers between devices, per_device(): lax.all_gather(flat_weight, 'row', axis=0, tiled=True)  158 us
    unnamed x2, blocking collectives  132 us
    all_gather x1, waiting for transfers between devices, per_device(): block_values = lax.all_gather(pair_values, 'tok', axis=0, tiled=True)  86.2 us
    dot_general x11, matrix products, update(): jnp.einsum('hqk,khd->qhd', weights, block_values, preferred_element_type=...  33 us
    dot_general x11, matrix products, update(): jnp.einsum('qhd,khd->hqk', query, block_keys, preferred_element_type=jnp....  21.6 us
    all_gather x1, waiting for transfers between devices, per_device(): lax.all_gather(activations, 'col', axis=1, tiled=True)  16.4 us
    reduce_sum x11, other arithmetic, update(): totals = totals * factor + jnp.sum(exponentials, axis=2)  10.7 us
  transfers between devices with their start and end apart: 4, of which 3 were waited for; matrix products, arithmetic and copies ran while one was open for 2% of the time, Pallas kernels for 0%

commit v1 on v0

v1 whole, which is shorter than its diff:
```python
import functools
import math

import jax
import jax.numpy as jnp
import numpy as np
from jax import lax
from jax.experimental import pallas as pl
from jax.experimental.pallas import tpu as pltpu
from jax.sharding import PartitionSpec as P

MESH = pl.DeviceIdType.MESH
F32 = jnp.float32
BF16 = jnp.bfloat16
NX, NY, NZ = 4, 4, 8
ROWS = 176
WIDTH = 1024
HALF = 2048
SUBS = 4
PIECE = 512 // SUBS
HIDE = -1e30
BIG = 1e9
PLUS = (0, 1)
MINUS = (3, 2)
ORDER = (0, 1, 3, 2)
SCALE = math.log2(math.e) / math.sqrt(128.0)


def kernel(
    x_ref, g_ref, w_ref, doc_ref, inv_ref, o_ref,
    xall, gall, wown, woth, cnt, cntall, bnd, xn, acc, cosb, sinb, stg, kv, qb, qcat, kaug,
    mrun, oacc, osend, obuf,
    lsem, wys, wyr, wzs, wzr, xs, xr, gs, gr, ps, pr, cs, cr, bs, br, as_, akr, aqr,
    rs, rp, rm, pks, pkr, os_, orr,
):
    t = lax.axis_index("tok")
    r = lax.axis_index("row")
    c = lax.axis_index("col")
    k = lax.rem(t, 2)
    yh = lax.rem(lax.div(t, 2), 2)
    z = lax.div(t, 4)
    y = yh * 2 + r
    zp = lax.rem(z, 2)

    def dev(cx, cy, cz, ck):
        return ((cz * 2 + lax.div(cy, 2)) * 2 + ck, lax.rem(cy, 2), cx)

    def xo(i):
        return lax.rem(c + i, NX)

    def yo(i):
        return lax.rem(y + i, NY)

    def zo(i):
        return lax.rem(z + i, NZ)

    partner = dev(c, y, z, 1 - k)
    pending = []

    def send(src, dst, ssem, rsem, to):
        copy = pltpu.make_async_remote_copy(
            src_ref=src, dst_ref=dst, send_sem=ssem, recv_sem=rsem,
            device_id=to, device_id_type=MESH,
        )
        copy.start()
        pending.append(copy)

    def landed(dst, rsem):
        pltpu.make_async_copy(dst, dst, rsem).wait()

    own_x = pltpu.make_async_copy(x_ref, xall.at[c, k], lsem.at[0])
    own_g = pltpu.make_async_copy(g_ref, gall.at[c], lsem.at[1])
    own_w = pltpu.make_async_copy(w_ref, wown, lsem.at[2])
    own_x.start()
    own_g.start()
    own_w.start()

    lane = lax.broadcasted_iota(jnp.int32, (1, 128), 1)
    ids = doc_ref[...]
    below = [jnp.sum((ids < d).astype(F32), axis=1, keepdims=True) for d in (1, 2, 3)]
    low = sum(jnp.where(lane == d + 1, below[d], 0.0) for d in range(3))
    high = sum(jnp.where(lane == d, below[d], 0.0) for d in range(3))
    sub = lax.broadcasted_iota(jnp.int32, (8, 128), 0)
    counts = jnp.where(sub == 0, low, jnp.where(sub == 1, high, 0.0))
    cnt[...] = counts
    cntall[0] = counts

    barrier = pltpu.get_barrier_semaphore()
    peers = [dev(xo(i), y, z, k) for i in (1, 2, 3)]
    peers += [dev(c, y, zo(1), k), dev(c, y, zo(NZ - 1), k)]
    plane = [(dy, dk) for dy in range(NY) for dk in range(2) if (dy, dk) != (0, 0)]
    core = (k, 1 - k)
    peers += [dev(c, yo(dy), z, core[dk]) for dy, dk in plane]
    for peer in peers:
        pl.semaphore_signal(barrier, inc=1, device_id=peer, device_id_type=MESH)
    pl.semaphore_wait(barrier, len(peers))

    yup, ydown = dev(c, yo(1), z, k), dev(c, yo(3), z, k)
    zup, zdown = dev(c, y, zo(1), k), dev(c, y, zo(NZ - 1), k)
    xup, xdown = dev(xo(1), y, z, k), dev(xo(3), y, z, k)
    for s in range(SUBS):
        for way, to in ((0, yup), (1, ydown)):
            off = way * 512 + s * PIECE
            send(
                w_ref.at[pl.ds(pl.multiple_of(zp * 1024 + off, PIECE), PIECE), :],
                woth.at[zp, pl.ds(off, PIECE), :],
                wys.at[way * SUBS + s], wyr.at[way * SUBS + s], to,
            )
        if s == 0:
            send(x_ref, xall.at[c, k], xs.at[0], xr.at[0], xup)
            send(x_ref, xall.at[c, k], xs.at[1], xr.at[1], xdown)
            send(x_ref, xall.at[c, k], ps.at[0], pr.at[0], partner)
            for i in (1, 2, 3):
                send(g_ref, gall.at[c], gs.at[i - 1], gr.at[NX - i - 1], dev(xo(i), y, z, k))
            for n, (dy, dk) in enumerate(plane):
                rel = ((NY - dy) % NY) * 2 + dk
                send(cnt, cntall.at[rel], cs.at[n], cr.at[rel - 1], dev(c, yo(dy), z, core[dk]))

    row = lax.broadcasted_iota(jnp.int32, (2 * ROWS, 128), 0)
    lanes = lax.broadcasted_iota(jnp.int32, (2 * ROWS, 128), 1)
    place = (z * 8 + yh * 4 + r) * ROWS + row + jnp.where(row >= ROWS, ROWS, 0)
    angle = place.astype(F32) * inv_ref[...]
    cosb[...] = jnp.cos(angle)
    sine = jnp.sin(angle)
    sinb[...] = jnp.where(lanes < 64, -sine, sine)

    for n in range(7):
        landed(cntall.at[n + 1], cr.at[n])
    total = cntall[0]
    for n in range(7):
        total = total + cntall[n + 1]
    lane8 = lax.broadcasted_iota(jnp.int32, (8, 128), 1)
    bnd[z] = jnp.where((sub == 1) & (lane8 >= 3), BIG, total)

    def forward_w(s):
        for way, to in ((0, zup), (1, zdown)):
            piece = woth.at[zp, pl.ds(way * 512 + s * PIECE, PIECE), :]
            landed(piece, wyr.at[way * SUBS + s])
            send(piece, piece, wzs.at[way * SUBS + s], wzr.at[way * SUBS + s], to)

    def bounds_hop(d):
        if d > 0:
            landed(bnd.at[zo(NZ - d)], br.at[2 * (d - 1)])
            if d < 4:
                landed(bnd.at[zo(d)], br.at[2 * (d - 1) + 1])
        if d < 4:
            send(bnd.at[zo(NZ - d)], bnd.at[zo(NZ - d)], bs.at[2 * d], br.at[2 * d], zup)
        if d < 3:
            send(bnd.at[zo(d)], bnd.at[zo(d)], bs.at[2 * d + 1], br.at[2 * d + 1], zdown)

    forward_w(0)
    bounds_hop(0)
    left, right, far = xo(3), xo(1), xo(2)
    landed(xall.at[left, k], xr.at[0])
    part = xall.at[left, k, pl.ds(0, 96), :]
    send(part, part, xs.at[2], xr.at[2], xup)
    send(xall.at[left, k], xall.at[left, k], ps.at[1], pr.at[1], partner)
    landed(xall.at[right, k], xr.at[1])
    part = xall.at[right, k, pl.ds(96, 80), :]
    send(part, part, xs.at[3], xr.at[3], xdown)
    send(xall.at[right, k], xall.at[right, k], ps.at[2], pr.at[2], partner)
    forward_w(1)
    bounds_hop(1)
    landed(xall.at[far, k, pl.ds(0, 96), :], xr.at[2])
    landed(xall.at[far, k, pl.ds(96, 80), :], xr.at[3])
    send(xall.at[far, k], xall.at[far, k], ps.at[3], pr.at[3], partner)
    forward_w(2)
    bounds_hop(2)

    own_x.wait()
    own_g.wait()
    for i in (1, 2, 3):
        landed(gall.at[xo(i)], gr.at[i - 1])
    for n, block in enumerate((c, left, right, far)):
        landed(xall.at[block, 1 - k], pr.at[n])
    for kk in range(2):
        squares = jnp.zeros((ROWS, 128), F32)
        for cc in range(NX):
            for s in range(8):
                v = xall[cc, kk, :, s * 128 : (s + 1) * 128].astype(F32)
                squares = squares + v * v
        mean = jnp.sum(squares, axis=1, keepdims=True) * (1.0 / (NX * WIDTH))
        inverse = jnp.broadcast_to(lax.rsqrt(mean + 1e-05), (ROWS, 128))
        for cc in range(NX):
            for s in range(8):
                v = xall[cc, kk, :, s * 128 : (s + 1) * 128].astype(F32)
                gain = gall[cc, s : s + 1, :].astype(F32)
                xn[cc, kk * ROWS : (kk + 1) * ROWS, s * 128 : (s + 1) * 128] = (
                    v * inverse * gain
                ).astype(BF16)
    forward_w(3)
    bounds_hop(3)

    own_w.wait()
    acc[...] = jnp.dot(xn[2 * r], wown[0:1024, :], preferred_element_type=F32)
    acc[...] += jnp.dot(xn[2 * r + 1], wown[1024:2048, :], preferred_element_type=F32)
    acc[...] += jnp.dot(xn[2 * (1 - r) + zp], woth[zp], preferred_element_type=F32)
    bounds_hop(4)
    for s in range(SUBS):
        for way in range(2):
            landed(
                woth.at[1 - zp, pl.ds(way * 512 + s * PIECE, PIECE), :],
                wzr.at[way * SUBS + s],
            )
    acc[...] += jnp.dot(xn[2 * (1 - r) + 1 - zp], woth[1 - zp], preferred_element_type=F32)

    def kv_at(p, zz, yy):
        return kv.at[p, zz, lax.div(yy, 2), pl.ds(0, 2), lax.rem(yy, 2)]

    cosine, sine = cosb[...], sinb[...]
    exchange = []
    for hh in range(2):
        for n in (1, 2, 0):
            u = acc[:, hh * 384 + n * 128 : hh * 384 + (n + 1) * 128]
            if n < 2:
                u = u * cosine + pltpu.roll(u, 64, 1) * sine
            stg[hh, n, 0] = u[:ROWS].astype(BF16)
            stg[hh, n, 1] = u[ROWS:].astype(BF16)
    for hh in range(2):
        yd = 2 * k + hh
        rel = lax.rem(y - yd + NY, NY)
        for j in range(2):
            here = jnp.logical_and(yd == y, k == j)
            to = dev(c, yd, z, j)
            moves = (
                (stg.at[hh, 1 + j], kv_at(j, z, y), as_.at[(hh * 2 + j) * 2], akr.at[rel]),
                (stg.at[hh, 0, j], qb.at[y], as_.at[(hh * 2 + j) * 2 + 1], aqr.at[rel]),
            )

            @pl.when(here)
            def _():
                for src, dst, _s, rsem in moves:
                    pltpu.make_async_copy(src, dst, rsem).start()

            @pl.when(jnp.logical_not(here))
            def _():
                for src, dst, ssem, rsem in moves:
                    pltpu.make_async_remote_copy(
                        src_ref=src, dst_ref=dst, send_sem=ssem, recv_sem=rsem,
                        device_id=to, device_id_type=MESH,
                    ).start()

            exchange.append((here, moves, to))

    for u in ORDER:
        block = kv_at(k, z, yo(u))
        landed(block, akr.at[u])
        send(block, block, rs.at[u], rp.at[u], zup)
        send(block, block, rs.at[4 + u], rm.at[u], zdown)
    send(kv.at[k, z], kv.at[k, z], pks.at[0], pkr.at[0], partner)

    mrun[...] = jnp.full_like(mrun, HIDE)
    oacc[...] = jnp.zeros_like(oacc)
    for u in ORDER:
        landed(qb.at[yo(u)], aqr.at[u])
    qrow = lax.broadcasted_iota(jnp.int32, (4 * ROWS, 128), 0)
    qplace = (qrow + jnp.where(qrow >= 2 * ROWS, 2 * ROWS, 0) + 2 * ROWS * k).astype(F32)
    mine = bnd[z]
    inside = (qplace >= mine[0:1, :]) & (qplace < mine[1:2, :])
    for n in range(4):
        qcat[n * ROWS : (n + 1) * ROWS, 0:128] = qb[n]
    qcat[:, 128:256] = jnp.where(inside, 1.0, 0.0).astype(BF16)

    def attend(zz, diagonal):
        limit = bnd[zz]
        krow = lax.broadcasted_iota(jnp.int32, (8 * ROWS, 128), 0).astype(F32)
        kin = (krow >= limit[0:1, :]) & (krow < limit[1:2, :])
        kaug[...] = jnp.where(kin, 0.0, HIDE).astype(BF16)

        def tile(i, carry):
            rows = pl.ds(pl.multiple_of(i * 2 * ROWS, 2 * ROWS), 2 * ROWS)
            keys = jnp.concatenate([kv[0, zz].reshape(8 * ROWS, 128), kaug[...]], axis=1)
            scores = lax.dot_general(
                qcat[rows, :], keys, (((1,), (1,)), ((), ())), preferred_element_type=F32
            ) * SCALE
            if diagonal:
                shape = (2 * ROWS, 8 * ROWS)
                qp = lax.broadcasted_iota(jnp.int32, shape, 0) + i * 4 * ROWS + 2 * ROWS * k
                kp = lax.broadcasted_iota(jnp.int32, shape, 1)
                scores = jnp.where(kp <= qp, scores, HIDE)
            before = mrun[rows, :]
            newest = jnp.maximum(before, jnp.max(scores, axis=1, keepdims=True))
            weights = jnp.exp2(scores - newest[:, 0:1]).astype(BF16)
            factor = jnp.exp2(before - newest)
            values = kv[1, zz].reshape(8 * ROWS, 128)
            values = jnp.concatenate([values, jnp.ones_like(values)], axis=1)
            added = jnp.dot(weights, values, preferred_element_type=F32)
            oacc[rows, :] = oacc[rows, :] * jnp.concatenate([factor, factor], axis=1) + added
            mrun[rows, :] = newest
            return carry

        lax.fori_loop(0, 2, tile, 0)

    landed(kv.at[1 - k, z], pkr.at[0])
    attend(z, True)

    for d in (1, 2, 3, 4):
        up, down = zo(NZ - d), zo(d)
        for u in ORDER:
            if d < 4 or u in PLUS:
                block = kv_at(k, up, yo(u))
                landed(block, rp.at[(d - 1) * 4 + u])
                if d < 3 or (d == 3 and u in PLUS):
                    send(block, block, rs.at[d * 8 + u], rp.at[d * 4 + u], zup)
            if d < 4 or u in MINUS:
                block = kv_at(k, down, yo(u))
                landed(block, rm.at[(d - 1) * 4 + u])
                if d < 3 or (d == 3 and u in MINUS):
                    send(block, block, rs.at[d * 8 + 4 + u], rm.at[d * 4 + u], zdown)
        send(kv.at[k, up], kv.at[k, up], pks.at[2 * d - 1], pkr.at[2 * d - 1], partner)
        if d < 4:
            send(kv.at[k, down], kv.at[k, down], pks.at[2 * d], pkr.at[2 * d], partner)
        landed(kv.at[1 - k, up], pkr.at[2 * d - 1])

        @pl.when(z >= d)
        def _():
            attend(up, False)

        if d < 4:
            landed(kv.at[1 - k, down], pkr.at[2 * d])

            @pl.when(z + d >= NZ)
            def _():
                attend(down, False)

    result = (oacc[:, 0:128] / oacc[:, 128:256]).astype(BF16)
    for n in range(4):
        osend[n] = result[n * ROWS : (n + 1) * ROWS]
    obuf[y] = osend[y]
    for dy in (1, 2, 3):
        send(osend.at[yo(dy)], obuf.at[y], os_.at[dy - 1], orr.at[NY - dy - 1], dev(c, yo(dy), z, k))
    for dy in (1, 2, 3):
        landed(obuf.at[yo(dy)], orr.at[dy - 1])
    for h in range(4):
        o_ref[:, h * 128 : (h + 1) * 128] = obuf[h]

    for here, moves, to in exchange:

        @pl.when(jnp.logical_not(here))
        def _():
            for src, dst, ssem, rsem in moves:
                pltpu.make_async_remote_copy(
                    src_ref=src, dst_ref=dst, send_sem=ssem, recv_sem=rsem,
                    device_id=to, device_id_type=MESH,
                ).wait_send()

    for copy in pending:
        copy.wait_send()


def per_device(activations, norm_gain, qkv_weight, doc_ids):
    core = lax.rem(lax.axis_index("tok"), 2)
    mine = lax.dynamic_slice_in_dim(qkv_weight, 2 * core, 2, axis=1).reshape(HALF, 768)
    spacing = np.arange(64).astype(np.float32) * np.float32(2.0 / 128)
    inverse = np.power(np.float32(10000.0), -spacing).astype(np.float32)
    inverse = np.concatenate([inverse, inverse])[None, :]
    dma = pltpu.SemaphoreType.DMA
    anywhere = pl.BlockSpec(memory_space=pl.ANY)
    local = pl.BlockSpec(memory_space=pltpu.VMEM)
    scratch = [
        pltpu.VMEM((NX, 2, ROWS, WIDTH), BF16),
        pltpu.VMEM((NX, 8, 128), BF16),
        pltpu.VMEM((HALF, 768), BF16),
        pltpu.VMEM((2, 1024, 768), BF16),
        pltpu.VMEM((8, 128), F32),
        pltpu.VMEM((8, 8, 128), F32),
        pltpu.VMEM((NZ, 8, 128), F32),
        pltpu.VMEM((NX, 2 * ROWS, WIDTH), BF16),
        pltpu.VMEM((2 * ROWS, 768), F32),
        pltpu.VMEM((2 * ROWS, 128), F32),
        pltpu.VMEM((2 * ROWS, 128), F32),
        pltpu.VMEM((2, 3, 2, ROWS, 128), BF16),
        pltpu.VMEM((2, NZ, 2, 2, 2, ROWS, 128), BF16),
        pltpu.VMEM((NY, ROWS, 128), BF16),
        pltpu.VMEM((4 * ROWS, 256), BF16),
        pltpu.VMEM((8 * ROWS, 128), BF16),
        pltpu.VMEM((4 * ROWS, 128), F32),
        pltpu.VMEM((4 * ROWS, 256), F32),
        pltpu.VMEM((NY, ROWS, 128), BF16),
        pltpu.VMEM((NY, ROWS, 128), BF16),
        dma((3,)),
        dma((2 * SUBS,)), dma((2 * SUBS,)),
        dma((2 * SUBS,)), dma((2 * SUBS,)),
        dma((4,)), dma((4,)),
        dma((3,)), dma((3,)),
        dma((4,)), dma((4,)),
        dma((7,)), dma((7,)),
        dma((8,)), dma((8,)),
        dma((8,)), dma((4,)), dma((4,)),
        dma((32,)), dma((16,)), dma((16,)),
        dma((8,)), dma((8,)),
        dma((3,)), dma((3,)),
    ]
    return pl.pallas_call(
        kernel,
        out_shape=jax.ShapeDtypeStruct((ROWS, 512), BF16),
        in_specs=[anywhere, anywhere, anywhere, local, local],
        out_specs=local,
        scratch_shapes=scratch,
        compiler_params=pltpu.CompilerParams(
            collective_id=0, has_side_effects=True, vmem_limit_bytes=60 * 1024 * 1024
        ),
        name="attention_block",
    )(
        activations, norm_gain.reshape(8, 128), mine, doc_ids.reshape(1, ROWS), jnp.asarray(inverse)
    )


def solution(mesh):
    placed = (P(("tok", "row"), "col"), P("col"), P("row", "col", None), P(("tok", "row")))
    return jax.shard_map(
        per_device, mesh=mesh, in_specs=placed, out_specs=P(("tok", "row"), "col"), check_vma=False
    )
```

time: 530 us -> 105 us (0.20)
  the two profiles are of different devices: /device:TPU:1 before, /device:TPU:225 now
where the time goes in v1:
time: 105 us; the launch traced here: 104 us
  Pallas kernels  85.1 us (81%)
  local copies, waits for them, and re-layouts  19.1 us (18%)
    pallas_call x1, Pallas kernels, per_device(): pl.pallas_call(kernel, out_shape=jax.ShapeDtypeStruct((ROWS, 512), BF16),...  85.1 us
    unnamed x2, local copies, waits for them, and re-layouts  8.45 us
    dynamic_slice x1, local copies, waits for them, and re-layouts, per_device(): lax.dynamic_slice_in_dim(qkv_weight, 2 * core, 2, axis=1).reshape(HALF, 768)  6.05 us
    reshape x1, local copies, waits for them, and re-layouts, per_device(): lax.dynamic_slice_in_dim(qkv_weight, 2 * core, 2, axis=1).reshape(HALF, 768)  4.64 us

profile of v1, /device:TPU:225, one launch (start us, length us, event | category | flops | bytes accessed | tf_op | source)
XLA Modules:
  0.0 104.3 jit_solution(12909022161942632121)
XLA Ops:
  0.0 6.0 %constant_dynamic-slice_fusion = bf16[2048,2,384]{2,1,0:T(2,128)(2,1)S(1)} fusion(bf16[2048,4,384]{2,1,0:T(4,128)(2,1)} %param.7, s32[]{:T(128)S(6)} %select_n.3), kind=kLoop, calls=%fused_computation | loop fusion | bytes 6291460 | tf_op jit(solution)/shard_map/dynamic_slice | solution.py:353
  6.1 6.8 %copy.8 = bf16[2048,2,384]{0,2,1:T(8,128)(2,1)} copy(bf16[2048,2,384]{2,1,0:T(2,128)(2,1)S(1)} %constant_dynamic-slice_fusion) | data formatting | bytes 6291456
  12.9 4.6 %copy.7.w_ref = bf16[2048,768]{1,0:T(8,128)(2,1)} copy(bf16[2048,768]{0,1:T(8,128)(2,1)} %bitcast.3) | data formatting | bytes 6291456 | tf_op jit(solution)/shard_map/reshape | solution.py:353
  17.5 85.1 %attention_block.1 = bf16[176,512]{1,0:T(8,128)(2,1)} custom-call(bf16[176,1024]{1,0:T(8,128)(2,1)} %x_ref.1, bf16[8,128]{1,0:T(8,128)(2,1)} %bitcast.4, bf16[2048,768]{1,0:T(8,128)(2,1)} %copy.7.w_ref, s32[1,176]{1,0:T(1,128)} %bitcast.5, f32[1,128]{1,0:T(1,128)} %constant.17.clone.inv_ref), custom_call_target="tpu_custom_call" | custom-call | tf_op jit(solution)/shard_map/attention_block/pallas_call | solution.py:394
  102.7 1.6 %copy.10 = bf16[176,512]{1,0:T(8,128)(2,1)} copy(bf16[176,512]{1,0:T(8,128)(2,1)} %attention_block.1) | data formatting | bytes 360448

commit v2 on v1

v2 whole, which is shorter than its diff:
```python
import functools
import math

import jax
import jax.numpy as jnp
import numpy as np
from jax import lax
from jax.experimental import pallas as pl
from jax.experimental.pallas import tpu as pltpu
from jax.sharding import PartitionSpec as P

MESH = pl.DeviceIdType.MESH
F32 = jnp.float32
BF16 = jnp.bfloat16
NX, NY, NZ = 4, 4, 8
ROWS = 176
WIDTH = 1024
HALF = 2048
SUBS = 4
PIECE = 512 // SUBS
QSUBS = 4
QPIECE = 1024 // QSUBS
HIDE = -1e30
BIG = 1e9
PLUS = (0, 1)
MINUS = (3, 2)
ORDER = (0, 1, 3, 2)
SCALE = math.log2(math.e) / math.sqrt(128.0)


def kernel(
    x_ref, g_ref, w_ref, doc_ref, inv_ref, o_ref,
    xall, gall, wkvo, wkvx, wqo, wqx, cnt, cntall, bnd, xn, acc, accq, cosb, sinb, stg, stgq, kv, qb, qcat, kaug,
    mrun, oacc, osend, obuf,
    lsem, wys, wyr, wzs, wzr, wqs, wqr, xs, xr, gs, gr, ps, pr, cs, cr, bs, br, as_, akr, aqs, aqr,
    rs, rp, rm, pks, pkr, os_, orr,
):
    t = lax.axis_index("tok")
    r = lax.axis_index("row")
    c = lax.axis_index("col")
    k = lax.rem(t, 2)
    yh = lax.rem(lax.div(t, 2), 2)
    z = lax.div(t, 4)
    y = yh * 2 + r
    zp = lax.rem(z, 2)

    def dev(cx, cy, cz, ck):
        return ((cz * 2 + lax.div(cy, 2)) * 2 + ck, lax.rem(cy, 2), cx)

    def xo(i):
        return lax.rem(c + i, NX)

    def yo(i):
        return lax.rem(y + i, NY)

    def zo(i):
        return lax.rem(z + i, NZ)

    partner = dev(c, y, z, 1 - k)
    pending = []

    def send(src, dst, ssem, rsem, to):
        copy = pltpu.make_async_remote_copy(
            src_ref=src, dst_ref=dst, send_sem=ssem, recv_sem=rsem,
            device_id=to, device_id_type=MESH,
        )
        copy.start()
        pending.append(copy)

    def landed(dst, rsem):
        pltpu.make_async_copy(dst, dst, rsem).wait()

    own_x = pltpu.make_async_copy(x_ref, xall.at[c, k], lsem.at[0])
    own_g = pltpu.make_async_copy(g_ref, gall.at[c], lsem.at[1])
    def q_columns(hh):
        return pl.ds(pl.multiple_of((2 * k + hh) * 384, 128), 128)

    def kv_columns(hh):
        return pl.ds(pl.multiple_of((2 * k + hh) * 384 + 128, 128), 256)

    own_w = []
    for hh in range(2):
        own_w.append(pltpu.make_async_copy(w_ref.at[:, kv_columns(hh)], wkvo.at[hh], lsem.at[2 + hh]))
    for hh in range(2):
        own_w.append(
            pltpu.make_async_copy(
                w_ref.at[:, q_columns(hh)], wqo.at[:, hh * 128 : (hh + 1) * 128], lsem.at[4 + hh]
            )
        )
    own_x.start()
    own_g.start()
    for copy in own_w:
        copy.start()

    lane = lax.broadcasted_iota(jnp.int32, (1, 128), 1)
    ids = doc_ref[...]
    below = [jnp.sum((ids < d).astype(F32), axis=1, keepdims=True) for d in (1, 2, 3)]
    low = sum(jnp.where(lane == d + 1, below[d], 0.0) for d in range(3))
    high = sum(jnp.where(lane == d, below[d], 0.0) for d in range(3))
    sub = lax.broadcasted_iota(jnp.int32, (8, 128), 0)
    counts = jnp.where(sub == 0, low, jnp.where(sub == 1, high, 0.0))
    cnt[...] = counts
    cntall[0] = counts

    barrier = pltpu.get_barrier_semaphore()
    peers = [dev(xo(i), y, z, k) for i in (1, 2, 3)]
    peers += [dev(c, y, zo(1), k), dev(c, y, zo(NZ - 1), k)]
    plane = [(dy, dk) for dy in range(NY) for dk in range(2) if (dy, dk) != (0, 0)]
    core = (k, 1 - k)
    peers += [dev(c, yo(dy), z, core[dk]) for dy, dk in plane]
    for peer in peers:
        pl.semaphore_signal(barrier, inc=1, device_id=peer, device_id_type=MESH)
    pl.semaphore_wait(barrier, len(peers))

    yup, ydown = dev(c, yo(1), z, k), dev(c, yo(3), z, k)
    zup, zdown = dev(c, y, zo(1), k), dev(c, y, zo(NZ - 1), k)
    xup, xdown = dev(xo(1), y, z, k), dev(xo(3), y, z, k)
    for i in (1, 2, 3):
        send(g_ref, gall.at[c], gs.at[i - 1], gr.at[NX - i - 1], dev(xo(i), y, z, k))
    for n, (dy, dk) in enumerate(plane):
        rel = ((NY - dy) % NY) * 2 + dk
        send(cnt, cntall.at[rel], cs.at[n], cr.at[rel - 1], dev(c, yo(dy), z, core[dk]))
    cuts = (pl.ds(0, 48), pl.ds(48, 48), pl.ds(96, 48), pl.ds(144, 32))

    def send_wkv(s):
        for hh in range(2):
            for way, to in ((0, yup), (1, ydown)):
                off = way * 512 + s * PIECE
                n = (way * SUBS + s) * 2 + hh
                send(
                    w_ref.at[pl.ds(pl.multiple_of(zp * 1024 + off, PIECE), PIECE), kv_columns(hh)],
                    wkvx.at[zp, hh, pl.ds(off, PIECE), :], wys.at[n], wyr.at[n], to,
                )

    def send_x(i):
        send(x_ref.at[cuts[i], :], xall.at[c, k, cuts[i], :], xs.at[i], xr.at[i], xup)
        i = 3 - i
        send(x_ref.at[cuts[i], :], xall.at[c, k, cuts[i], :], xs.at[4 + i], xr.at[4 + i], xdown)

    left, right, far = xo(3), xo(1), xo(2)

    def relay_x(i):
        part = xall.at[left, k, cuts[i], :]
        landed(part, xr.at[i])
        send(part, part, xs.at[8 + i], xr.at[8 + i], xup)
        i = 3 - i
        part = xall.at[right, k, cuts[i], :]
        landed(part, xr.at[4 + i])
        send(part, part, xs.at[8 + i], xr.at[8 + i], xdown)

    for i in range(2):
        send_wkv(i)
        send_x(i)
    send_x(2)
    send_x(3)
    send(x_ref, xall.at[c, k], ps.at[0], pr.at[0], partner)

    def send_wq(s):
        for way, to in ((0, yup), (1, ydown)):
            for hh in range(2):
                rows = pl.ds(way * 1024 + s * QPIECE, QPIECE)
                n = (way * QSUBS + s) * 2 + hh
                send(
                    w_ref.at[rows, q_columns(hh)], wqx.at[rows, hh * 128 : (hh + 1) * 128],
                    wqs.at[n], wqr.at[n], to,
                )

    row = lax.broadcasted_iota(jnp.int32, (2 * ROWS, 128), 0)
    lanes = lax.broadcasted_iota(jnp.int32, (2 * ROWS, 128), 1)
    place = (z * 8 + yh * 4 + r) * ROWS + row + jnp.where(row >= ROWS, ROWS, 0)
    angle = place.astype(F32) * inv_ref[...]
    cosb[...] = jnp.cos(angle)
    sine = jnp.sin(angle)
    sinb[...] = jnp.where(lanes < 64, -sine, sine)

    for n in range(7):
        landed(cntall.at[n + 1], cr.at[n])
    total = cntall[0]
    for n in range(7):
        total = total + cntall[n + 1]
    lane8 = lax.broadcasted_iota(jnp.int32, (8, 128), 1)
    bnd[z] = jnp.where((sub == 1) & (lane8 >= 3), BIG, total)

    def forward_w(s):
        for way, to in ((0, zup), (1, zdown)):
            rows = pl.ds(way * 512 + s * PIECE, PIECE)
            for hh in range(2):
                landed(wkvx.at[zp, hh, rows, :], wyr.at[(way * SUBS + s) * 2 + hh])
            piece = wkvx.at[zp, pl.ds(0, 2), rows, :]
            send(piece, piece, wzs.at[way * SUBS + s], wzr.at[way * SUBS + s], to)

    def bounds_hop(d):
        if d > 0:
            landed(bnd.at[zo(NZ - d)], br.at[2 * (d - 1)])
            if d < 4:
                landed(bnd.at[zo(d)], br.at[2 * (d - 1) + 1])
        if d < 4:
            send(bnd.at[zo(NZ - d)], bnd.at[zo(NZ - d)], bs.at[2 * d], br.at[2 * d], zup)
        if d < 3:
            send(bnd.at[zo(d)], bnd.at[zo(d)], bs.at[2 * d + 1], br.at[2 * d + 1], zdown)

    forward_w(0)
    send_wkv(2)
    bounds_hop(0)
    relay_x(0)
    relay_x(1)
    forward_w(1)
    send_wkv(3)
    bounds_hop(1)
    for i in (2, 3):
        landed(xall.at[left, k, cuts[i], :], xr.at[i])
        landed(xall.at[right, k, cuts[3 - i], :], xr.at[7 - i])
    send(xall.at[left, k], xall.at[left, k], ps.at[1], pr.at[1], partner)
    send(xall.at[right, k], xall.at[right, k], ps.at[2], pr.at[2], partner)
    forward_w(2)
    send_wq(0)
    bounds_hop(2)
    for i in range(4):
        landed(xall.at[far, k, cuts[i], :], xr.at[8 + i])
    send(xall.at[far, k], xall.at[far, k], ps.at[3], pr.at[3], partner)
    own_x.wait()
    own_g.wait()
    for i in (1, 2, 3):
        landed(gall.at[xo(i)], gr.at[i - 1])

    def normalise(kk, at):
        squares = jnp.zeros((ROWS, 128), F32)
        for cc in range(NX):
            for s in range(8):
                v = xall[cc, kk, :, s * 128 : (s + 1) * 128].astype(F32)
                squares = squares + v * v
        mean = jnp.sum(squares, axis=1, keepdims=True) * (1.0 / (NX * WIDTH))
        inverse = jnp.broadcast_to(lax.rsqrt(mean + 1e-05), (ROWS, 128))
        for cc in range(NX):
            for s in range(8):
                v = xall[cc, kk, :, s * 128 : (s + 1) * 128].astype(F32)
                gain = gall[cc, s : s + 1, :].astype(F32)
                xn[cc, at, s * 128 : (s + 1) * 128] = (v * inverse * gain).astype(BF16)

    normalise(k, pl.ds(pl.multiple_of(k * ROWS, ROWS), ROWS))
    forward_w(3)
    send_wq(1)
    bounds_hop(3)
    for n, block in enumerate((c, left, right, far)):
        landed(xall.at[block, 1 - k], pr.at[n])
    normalise(1 - k, pl.ds(pl.multiple_of((1 - k) * ROWS, ROWS), ROWS))
    for hh in range(2):
        own_w[hh].wait()
        out = slice(hh * 256, (hh + 1) * 256)
        acc[:, out] = jnp.dot(xn[2 * r], wkvo[hh, 0:1024], preferred_element_type=F32)
        acc[:, out] += jnp.dot(xn[2 * r + 1], wkvo[hh, 1024:2048], preferred_element_type=F32)
        acc[:, out] += jnp.dot(xn[2 * (1 - r) + zp], wkvx[zp, hh], preferred_element_type=F32)
    bounds_hop(4)
    for s in range(SUBS):
        for way in range(2):
            landed(
                wkvx.at[1 - zp, pl.ds(0, 2), pl.ds(way * 512 + s * PIECE, PIECE), :],
                wzr.at[way * SUBS + s],
            )
    for hh in range(2):
        out = slice(hh * 256, (hh + 1) * 256)
        acc[:, out] += jnp.dot(xn[2 * (1 - r) + 1 - zp], wkvx[1 - zp, hh], preferred_element_type=F32)

    def kv_at(p, zz, yy):
        return kv.at[p, zz, lax.div(yy, 2), pl.ds(0, 2), lax.rem(yy, 2)]

    for hh in range(2):
        u = acc[:, hh * 256 : hh * 256 + 128]
        u = u * cosb[...] + pltpu.roll(u, 64, 1) * sinb[...]
        stg[hh, 0, 0] = u[:ROWS].astype(BF16)
        stg[hh, 0, 1] = u[ROWS:].astype(BF16)
        u = acc[:, hh * 256 + 128 : hh * 256 + 256]
        stg[hh, 1, 0] = u[:ROWS].astype(BF16)
        stg[hh, 1, 1] = u[ROWS:].astype(BF16)
    exchange = []

    def exchange_send(source, slot_of, ssems, rsems):
        for hh in range(2):
            yd = 2 * k + hh
            rel = lax.rem(y - yd + NY, NY)
            for j in range(2):
                here = jnp.logical_and(yd == y, k == j)
                to = dev(c, yd, z, j)
                move = (source.at[hh, j], slot_of(j), ssems.at[hh * 2 + j], rsems.at[rel])

                @pl.when(here)
                def _():
                    pltpu.make_async_copy(move[0], move[1], move[3]).start()

                @pl.when(jnp.logical_not(here))
                def _():
                    pltpu.make_async_remote_copy(
                        src_ref=move[0], dst_ref=move[1], send_sem=move[2], recv_sem=move[3],
                        device_id=to, device_id_type=MESH,
                    ).start()

                exchange.append((here, move, to))

    exchange_send(stg, lambda j: kv_at(j, z, y), as_, akr)
    send_wq(2)
    send_wq(3)

    own_w[2].wait()
    own_w[3].wait()
    accq[...] = jnp.dot(xn[2 * r], wqo[0:1024, :], preferred_element_type=F32)
    accq[...] += jnp.dot(xn[2 * r + 1], wqo[1024:2048, :], preferred_element_type=F32)

    def project_q(part):
        for s in (2 * part, 2 * part + 1):
            for way in range(2):
                for hh in range(2):
                    landed(
                        wqx.at[pl.ds(way * 1024 + s * QPIECE, QPIECE), hh * 128 : (hh + 1) * 128],
                        wqr.at[(way * QSUBS + s) * 2 + hh],
                    )
        low = part * 512
        for way in range(2):
            accq[...] += jnp.dot(
                xn[2 * (1 - r) + way, :, low : low + 512],
                wqx[way * 1024 + low : way * 1024 + low + 512, :],
                preferred_element_type=F32,
            )

    project_q(0)
    for u in ORDER:
        block = kv_at(k, z, yo(u))
        landed(block, akr.at[u])
        send(block, block, rs.at[u], rp.at[u], zup)
        send(block, block, rs.at[4 + u], rm.at[u], zdown)
        send(block, block, pks.at[u], pkr.at[u], partner)

    def ring(d, pieces):
        up, down = zo(NZ - d), zo(d)
        for u in pieces:
            if d < 4 or u in PLUS:
                block = kv_at(k, up, yo(u))
                landed(block, rp.at[(d - 1) * 4 + u])
                if d < 3 or (d == 3 and u in PLUS):
                    send(block, block, rs.at[d * 8 + u], rp.at[d * 4 + u], zup)
                n = (2 * d - 1) * 4 + u
                send(block, block, pks.at[n], pkr.at[n], partner)
            if d < 4 or u in MINUS:
                block = kv_at(k, down, yo(u))
                landed(block, rm.at[(d - 1) * 4 + u])
                if d < 3 or (d == 3 and u in MINUS):
                    send(block, block, rs.at[d * 8 + 4 + u], rm.at[d * 4 + u], zdown)
                n = (2 * d if d < 4 else 7) * 4 + u
                send(block, block, pks.at[n], pkr.at[n], partner)
    project_q(1)
    for hh in range(2):
        u = accq[:, hh * 128 : (hh + 1) * 128]
        u = u * cosb[...] + pltpu.roll(u, 64, 1) * sinb[...]
        stgq[hh, 0] = u[:ROWS].astype(BF16)
        stgq[hh, 1] = u[ROWS:].astype(BF16)
    exchange_send(stgq, lambda j: qb.at[y], aqs, aqr)

    ring(1, ORDER)

    mrun[...] = jnp.full_like(mrun, HIDE)
    oacc[...] = jnp.zeros_like(oacc)
    qrow = lax.broadcasted_iota(jnp.int32, (4 * ROWS, 128), 0)
    qplace = (qrow + jnp.where(qrow >= 2 * ROWS, 2 * ROWS, 0) + 2 * ROWS * k).astype(F32)
    mine = bnd[z]
    inside = (qplace >= mine[0:1, :]) & (qplace < mine[1:2, :])
    qcat[:, 128:256] = jnp.where(inside, 1.0, 0.0).astype(BF16)
    for u in ORDER:
        landed(qb.at[yo(u)], aqr.at[u])
    for n in range(4):
        qcat[n * ROWS : (n + 1) * ROWS, 0:128] = qb[n]

    def attend(zz, diagonal):
        limit = bnd[zz]
        krow = lax.broadcasted_iota(jnp.int32, (8 * ROWS, 128), 0).astype(F32)
        kin = (krow >= limit[0:1, :]) & (krow < limit[1:2, :])
        kaug[...] = jnp.where(kin, 0.0, HIDE).astype(BF16)

        keys = jnp.concatenate([kv[0, zz].reshape(8 * ROWS, 128), kaug[...]], axis=1)
        values = kv[1, zz].reshape(8 * ROWS, 128)
        values = jnp.concatenate([values, jnp.ones_like(values)], axis=1)

        def scored(i):
            rows = slice(i * 2 * ROWS, (i + 1) * 2 * ROWS)
            return lax.dot_general(
                qcat[rows, :], keys, (((1,), (1,)), ((), ())), preferred_element_type=F32
            )

        def absorb(i, scores):
            rows = slice(i * 2 * ROWS, (i + 1) * 2 * ROWS)
            if diagonal:
                shape = (2 * ROWS, 8 * ROWS)
                qp = lax.broadcasted_iota(jnp.int32, shape, 0) + i * 4 * ROWS + 2 * ROWS * k
                kp = lax.broadcasted_iota(jnp.int32, shape, 1)
                scores = jnp.where(kp <= qp, scores, HIDE)
            before = mrun[rows, :]
            newest = jnp.maximum(before, jnp.max(scores, axis=1, keepdims=True))
            weights = jnp.exp2((scores - newest[:, 0:1]) * SCALE).astype(BF16)
            factor = jnp.exp2((before - newest) * SCALE)
            added = jnp.dot(weights, values, preferred_element_type=F32)
            oacc[rows, :] = oacc[rows, :] * jnp.concatenate([factor, factor], axis=1) + added
            mrun[rows, :] = newest

        first = scored(0)
        second = scored(1)
        absorb(0, first)
        absorb(1, second)

    def shared(zz, n):
        for u in ORDER:
            landed(kv_at(1 - k, zz, yo(u)), pkr.at[n * 4 + u])

    def attend_up(d):
        shared(zo(NZ - d), 2 * d - 1)

        @pl.when(z >= d)
        def _():
            attend(zo(NZ - d), False)

    def attend_down(d):
        shared(zo(d), 2 * d)

        @pl.when(z + d >= NZ)
        def _():
            attend(zo(d), False)

    shared(z, 0)
    attend(z, True)
    ring(2, ORDER)
    attend_up(1)
    attend_down(1)
    ring(3, ORDER[:2])
    attend_up(2)
    ring(3, ORDER[2:])
    attend_down(2)
    ring(4, ORDER)
    attend_up(3)
    attend_down(3)
    attend_up(4)

    result = (oacc[:, 0:128] / oacc[:, 128:256]).astype(BF16)
    for n in range(4):
        osend[n] = result[n * ROWS : (n + 1) * ROWS]
    obuf[y] = osend[y]
    for dy in (1, 2, 3):
        send(osend.at[yo(dy)], obuf.at[y], os_.at[dy - 1], orr.at[NY - dy - 1], dev(c, yo(dy), z, k))
    for dy in (1, 2, 3):
        landed(obuf.at[yo(dy)], orr.at[dy - 1])
    for h in range(4):
        o_ref[:, h * 128 : (h + 1) * 128] = obuf[h]

    for here, move, to in exchange:

        @pl.when(jnp.logical_not(here))
        def _():
            pltpu.make_async_remote_copy(
                src_ref=move[0], dst_ref=move[1], send_sem=move[2], recv_sem=move[3],
                device_id=to, device_id_type=MESH,
            ).wait_send()

    for copy in pending:
        copy.wait_send()


def per_device(activations, norm_gain, qkv_weight, doc_ids):
    mine = qkv_weight.reshape(HALF, 1536)
    spacing = np.arange(64).astype(np.float32) * np.float32(2.0 / 128)
    inverse = np.power(np.float32(10000.0), -spacing).astype(np.float32)
    inverse = np.concatenate([inverse, inverse])[None, :]
    dma = pltpu.SemaphoreType.DMA
    anywhere = pl.BlockSpec(memory_space=pl.ANY)
    local = pl.BlockSpec(memory_space=pltpu.VMEM)
    scratch = [
        pltpu.VMEM((NX, 2, ROWS, WIDTH), BF16),
        pltpu.VMEM((NX, 8, 128), BF16),
        pltpu.VMEM((2, HALF, 256), BF16),
        pltpu.VMEM((2, 2, 1024, 256), BF16),
        pltpu.VMEM((HALF, 256), BF16),
        pltpu.VMEM((HALF, 256), BF16),
        pltpu.VMEM((8, 128), F32),
        pltpu.VMEM((8, 8, 128), F32),
        pltpu.VMEM((NZ, 8, 128), F32),
        pltpu.VMEM((NX, 2 * ROWS, WIDTH), BF16),
        pltpu.VMEM((2 * ROWS, 512), F32),
        pltpu.VMEM((2 * ROWS, 256), F32),
        pltpu.VMEM((2 * ROWS, 128), F32),
        pltpu.VMEM((2 * ROWS, 128), F32),
        pltpu.VMEM((2, 2, 2, ROWS, 128), BF16),
        pltpu.VMEM((2, 2, ROWS, 128), BF16),
        pltpu.VMEM((2, NZ, 2, 2, 2, ROWS, 128), BF16),
        pltpu.VMEM((NY, ROWS, 128), BF16),
        pltpu.VMEM((4 * ROWS, 256), BF16),
        pltpu.VMEM((8 * ROWS, 128), BF16),
        pltpu.VMEM((4 * ROWS, 128), F32),
        pltpu.VMEM((4 * ROWS, 256), F32),
        pltpu.VMEM((NY, ROWS, 128), BF16),
        pltpu.VMEM((NY, ROWS, 128), BF16),
        dma((6,)),
        dma((4 * SUBS,)), dma((4 * SUBS,)),
        dma((2 * SUBS,)), dma((2 * SUBS,)),
        dma((4 * QSUBS,)), dma((4 * QSUBS,)),
        dma((12,)), dma((12,)),
        dma((3,)), dma((3,)),
        dma((4,)), dma((4,)),
        dma((7,)), dma((7,)),
        dma((8,)), dma((8,)),
        dma((4,)), dma((4,)), dma((4,)), dma((4,)),
        dma((32,)), dma((16,)), dma((16,)),
        dma((32,)), dma((32,)),
        dma((3,)), dma((3,)),
    ]
    return pl.pallas_call(
        kernel,
        out_shape=jax.ShapeDtypeStruct((ROWS, 512), BF16),
        in_specs=[anywhere, anywhere, anywhere, local, local],
        out_specs=local,
        scratch_shapes=scratch,
        compiler_params=pltpu.CompilerParams(
            collective_id=0, has_side_effects=True, vmem_limit_bytes=60 * 1024 * 1024
        ),
        name="attention_block",
    )(
        activations, norm_gain.reshape(8, 128), mine, doc_ids.reshape(1, ROWS), jnp.asarray(inverse)
    )


def solution(mesh):
    placed = (P(("tok", "row"), "col"), P("col"), P("row", "col", None), P(("tok", "row")))
    return jax.shard_map(
        per_device, mesh=mesh, in_specs=placed, out_specs=P(("tok", "row"), "col"), check_vma=False
    )
```

time: 105 us -> 82.1 us (0.78)
  the two profiles are of different devices: /device:TPU:225 before, /device:TPU:1 now
where the time goes in v2:
time: 82.1 us; the launch traced here: 82 us
  Pallas kernels  73.7 us (90%)
  local copies, waits for them, and re-layouts  8.22 us (10%)
    pallas_call x1, Pallas kernels, per_device(): pl.pallas_call(kernel, out_shape=jax.ShapeDtypeStruct((ROWS, 512), BF16),...  73.7 us
    unnamed x2, local copies, waits for them, and re-layouts  8.22 us

profile of v2, /device:TPU:1, one launch (start us, length us, event | category | flops | bytes accessed | tf_op | source)
XLA Modules:
  0.0 82.0 jit_solution(2167072482488324386)
XLA Ops:
  0.0 6.6 %copy.6 = bf16[256,8,4,384]{3,1,2,0:T(8,128)(2,1)} copy(bf16[256,8,4,384]{3,2,1,0:T(4,128)(2,1)} %bitcast.5) | data formatting | bytes 12582912
  6.6 73.7 %attention_block.1 = bf16[176,512]{1,0:T(8,128)(2,1)} custom-call(bf16[176,1024]{1,0:T(8,128)(2,1)} %x_ref.1, bf16[8,128]{1,0:T(8,128)(2,1)} %bitcast.6, bf16[2048,1536]{1,0:T(8,128)(2,1)} %bitcast.4, s32[1,176]{1,0:T(1,128)} %bitcast.7, f32[1,128]{1,0:T(1,128)} %constant.2.clone.inv_ref), custom_call_target="tpu_custom_call" | custom-call | tf_op jit(solution)/shard_map/attention_block/pallas_call | solution.py:510
  80.3 1.6 %copy.8 = bf16[176,512]{1,0:T(8,128)(2,1)} copy(bf16[176,512]{1,0:T(8,128)(2,1)} %attention_block.1) | data formatting | bytes 360448

commit v3 on v2

--- a/solution.py
+++ b/solution.py
@@ -30,7 +30,7 @@
 
 def kernel(
     x_ref, g_ref, w_ref, doc_ref, inv_ref, o_ref,
-    xall, gall, wkvo, wkvx, wqo, wqx, cnt, cntall, bnd, xn, acc, accq, cosb, sinb, stg, stgq, kv, qb, qcat, kaug,
+    xall, gall, raw, wkvo, wkvx, wqo, wqx, cnt, cntall, bnd, xn, acc, accq, cosb, sinb, stg, stgq, kv, qb, qcat, kaug,
     mrun, oacc, osend, obuf,
     lsem, wys, wyr, wzs, wzr, wqs, wqr, xs, xr, gs, gr, ps, pr, cs, cr, bs, br, as_, akr, aqs, aqr,
     rs, rp, rm, pks, pkr, os_, orr,
@@ -72,25 +72,29 @@
 
     own_x = pltpu.make_async_copy(x_ref, xall.at[c, k], lsem.at[0])
     own_g = pltpu.make_async_copy(g_ref, gall.at[c], lsem.at[1])
-    def q_columns(hh):
-        return pl.ds(pl.multiple_of((2 * k + hh) * 384, 128), 128)
-
-    def kv_columns(hh):
-        return pl.ds(pl.multiple_of((2 * k + hh) * 384 + 128, 128), 256)
-
-    own_w = []
-    for hh in range(2):
-        own_w.append(pltpu.make_async_copy(w_ref.at[:, kv_columns(hh)], wkvo.at[hh], lsem.at[2 + hh]))
-    for hh in range(2):
-        own_w.append(
-            pltpu.make_async_copy(
-                w_ref.at[:, q_columns(hh)], wqo.at[:, hh * 128 : (hh + 1) * 128], lsem.at[4 + hh]
-            )
-        )
+    def raw_rows(n):
+        half = zp if n < 8 else 1 - zp
+        off = (n % 2) * 512 + (n % 8) // 2 * 128
+        return pl.ds(pl.multiple_of(half * 1024 + off, 128), 128)
+
+    raw_copies = [
+        pltpu.make_async_copy(w_ref.at[raw_rows(n)], raw.at[raw_rows(n)], lsem.at[2 + n])
+        for n in range(16)
+    ]
+    for copy in raw_copies:
+        copy.start()
     own_x.start()
     own_g.start()
-    for copy in own_w:
-        copy.start()
+
+    def unpack_w(n):
+        raw_copies[n].wait()
+        rows = raw_rows(n)
+        heads = jnp.swapaxes(raw[rows], 0, 1)
+        for hh in range(2):
+            head = jnp.where(k == 0, heads[hh], heads[2 + hh])
+            wqo[rows, hh * 128 : (hh + 1) * 128] = head[:, 0:128]
+            wkvo[hh, rows, :] = head[:, 128:384]
+
 
     lane = lax.broadcasted_iota(jnp.int32, (1, 128), 1)
     ids = doc_ref[...]
@@ -110,6 +114,8 @@
     peers += [dev(c, yo(dy), z, core[dk]) for dy, dk in plane]
     for peer in peers:
         pl.semaphore_signal(barrier, inc=1, device_id=peer, device_id_type=MESH)
+    unpack_w(0)
+    unpack_w(1)
     pl.semaphore_wait(barrier, len(peers))
 
     yup, ydown = dev(c, yo(1), z, k), dev(c, yo(3), z, k)
@@ -123,14 +129,13 @@
     cuts = (pl.ds(0, 48), pl.ds(48, 48), pl.ds(96, 48), pl.ds(144, 32))
 
     def send_wkv(s):
-        for hh in range(2):
-            for way, to in ((0, yup), (1, ydown)):
-                off = way * 512 + s * PIECE
-                n = (way * SUBS + s) * 2 + hh
-                send(
-                    w_ref.at[pl.ds(pl.multiple_of(zp * 1024 + off, PIECE), PIECE), kv_columns(hh)],
-                    wkvx.at[zp, hh, pl.ds(off, PIECE), :], wys.at[n], wyr.at[n], to,
-                )
+        for way, to in ((0, yup), (1, ydown)):
+            off = way * 512 + s * PIECE
+            send(
+                wkvo.at[pl.ds(0, 2), pl.ds(pl.multiple_of(zp * 1024 + off, PIECE), PIECE), :],
+                wkvx.at[zp, pl.ds(0, 2), pl.ds(off, PIECE), :],
+                wys.at[way * SUBS + s], wyr.at[way * SUBS + s], to,
+            )
 
     def send_x(i):
         send(x_ref.at[cuts[i], :], xall.at[c, k, cuts[i], :], xs.at[i], xr.at[i], xup)
@@ -148,22 +153,26 @@
         landed(part, xr.at[4 + i])
         send(part, part, xs.at[8 + i], xr.at[8 + i], xdown)
 
-    for i in range(2):
-        send_wkv(i)
-        send_x(i)
+    send_x(0)
+    unpack_w(2)
+    unpack_w(3)
+    send_wkv(0)
+    send_x(1)
+    unpack_w(4)
+    unpack_w(5)
+    send_wkv(1)
     send_x(2)
     send_x(3)
     send(x_ref, xall.at[c, k], ps.at[0], pr.at[0], partner)
 
     def send_wq(s):
         for way, to in ((0, yup), (1, ydown)):
-            for hh in range(2):
-                rows = pl.ds(way * 1024 + s * QPIECE, QPIECE)
-                n = (way * QSUBS + s) * 2 + hh
-                send(
-                    w_ref.at[rows, q_columns(hh)], wqx.at[rows, hh * 128 : (hh + 1) * 128],
-                    wqs.at[n], wqr.at[n], to,
-                )
+            rows = pl.ds(way * 1024 + s * QPIECE, QPIECE)
+            n = way * QSUBS + s
+            send(wqo.at[rows, :], wqx.at[rows, :], wqs.at[n], wqr.at[n], to)
+
+    for n in range(6, 16):
+        unpack_w(n)
 
     row = lax.broadcasted_iota(jnp.int32, (2 * ROWS, 128), 0)
     lanes = lax.broadcasted_iota(jnp.int32, (2 * ROWS, 128), 1)
@@ -184,9 +193,8 @@
     def forward_w(s):
         for way, to in ((0, zup), (1, zdown)):
             rows = pl.ds(way * 512 + s * PIECE, PIECE)
-            for hh in range(2):
-                landed(wkvx.at[zp, hh, rows, :], wyr.at[(way * SUBS + s) * 2 + hh])
             piece = wkvx.at[zp, pl.ds(0, 2), rows, :]
+            landed(piece, wyr.at[way * SUBS + s])
             send(piece, piece, wzs.at[way * SUBS + s], wzr.at[way * SUBS + s], to)
 
     def bounds_hop(d):
@@ -245,7 +253,6 @@
         landed(xall.at[block, 1 - k], pr.at[n])
     normalise(1 - k, pl.ds(pl.multiple_of((1 - k) * ROWS, ROWS), ROWS))
     for hh in range(2):
-        own_w[hh].wait()
         out = slice(hh * 256, (hh + 1) * 256)
         acc[:, out] = jnp.dot(xn[2 * r], wkvo[hh, 0:1024], preferred_element_type=F32)
         acc[:, out] += jnp.dot(xn[2 * r + 1], wkvo[hh, 1024:2048], preferred_element_type=F32)
@@ -300,19 +307,15 @@
     send_wq(2)
     send_wq(3)
 
-    own_w[2].wait()
-    own_w[3].wait()
     accq[...] = jnp.dot(xn[2 * r], wqo[0:1024, :], preferred_element_type=F32)
     accq[...] += jnp.dot(xn[2 * r + 1], wqo[1024:2048, :], preferred_element_type=F32)
 
     def project_q(part):
         for s in (2 * part, 2 * part + 1):
             for way in range(2):
-                for hh in range(2):
-                    landed(
-                        wqx.at[pl.ds(way * 1024 + s * QPIECE, QPIECE), hh * 128 : (hh + 1) * 128],
-                        wqr.at[(way * QSUBS + s) * 2 + hh],
-                    )
+                landed(
+                    wqx.at[pl.ds(way * 1024 + s * QPIECE, QPIECE), :], wqr.at[way * QSUBS + s]
+                )
         low = part * 512
         for way in range(2):
             accq[...] += jnp.dot(
@@ -461,7 +464,6 @@
 
 
 def per_device(activations, norm_gain, qkv_weight, doc_ids):
-    mine = qkv_weight.reshape(HALF, 1536)
     spacing = np.arange(64).astype(np.float32) * np.float32(2.0 / 128)
     inverse = np.power(np.float32(10000.0), -spacing).astype(np.float32)
     inverse = np.concatenate([inverse, inverse])[None, :]
@@ -471,6 +473,7 @@
     scratch = [
         pltpu.VMEM((NX, 2, ROWS, WIDTH), BF16),
         pltpu.VMEM((NX, 8, 128), BF16),
+        pltpu.VMEM((HALF, 4, 384), BF16),
         pltpu.VMEM((2, HALF, 256), BF16),
         pltpu.VMEM((2, 2, 1024, 256), BF16),
         pltpu.VMEM((HALF, 256), BF16),
@@ -493,10 +496,10 @@
         pltpu.VMEM((4 * ROWS, 256), F32),
         pltpu.VMEM((NY, ROWS, 128), BF16),
         pltpu.VMEM((NY, ROWS, 128), BF16),
-        dma((6,)),
-        dma((4 * SUBS,)), dma((4 * SUBS,)),
+        dma((18,)),
         dma((2 * SUBS,)), dma((2 * SUBS,)),
-        dma((4 * QSUBS,)), dma((4 * QSUBS,)),
+        dma((2 * SUBS,)), dma((2 * SUBS,)),
+        dma((2 * QSUBS,)), dma((2 * QSUBS,)),
         dma((12,)), dma((12,)),
         dma((3,)), dma((3,)),
         dma((4,)), dma((4,)),
@@ -518,7 +521,7 @@
         ),
         name="attention_block",
     )(
-        activations, norm_gain.reshape(8, 128), mine, doc_ids.reshape(1, ROWS), jnp.asarray(inverse)
+        activations, norm_gain.reshape(8, 128), qkv_weight, doc_ids.reshape(1, ROWS), jnp.asarray(inverse)
     )
 
 

time: 82.1 us -> 75.3 us (0.917)
  local copies, waits for them, and re-layouts: 8.22 us -> 1.61 us
    unnamed x2 -> x1, local copies, waits for them, and re-layouts: 8.22 us -> 1.61 us
where the time goes in v3:
time: 75.3 us; the launch traced here: 75.2 us
  Pallas kernels  73.5 us (98%)
  local copies, waits for them, and re-layouts  1.61 us (2%)
    pallas_call x1, Pallas kernels, per_device(): pl.pallas_call(kernel, out_shape=jax.ShapeDtypeStruct((ROWS, 512), BF16),...  73.5 us
    unnamed x1, local copies, waits for them, and re-layouts  1.61 us

profile of v3, /device:TPU:1, one launch (start us, length us, event | category | flops | bytes accessed | tf_op | source)
XLA Modules:
  0.0 75.2 jit_solution(1232427539964833471)
XLA Ops:
  0.0 73.5 %attention_block.1 = bf16[176,512]{1,0:T(8,128)(2,1)} custom-call(bf16[176,1024]{1,0:T(8,128)(2,1)} %x_ref.1, bf16[8,128]{1,0:T(8,128)(2,1)} %bitcast.2, bf16[2048,4,384]{2,1,0:T(4,128)(2,1)} %w_ref.1, s32[1,176]{1,0:T(1,128)} %bitcast.3, f32[1,128]{1,0:T(1,128)} %constant.2.clone.inv_ref), custom_call_target="tpu_custom_call" | custom-call | tf_op jit(solution)/shard_map/attention_block/pallas_call | solution.py:513
  73.6 1.6 %copy.7 = bf16[176,512]{1,0:T(8,128)(2,1)} copy(bf16[176,512]{1,0:T(8,128)(2,1)} %attention_block.1) | data formatting | bytes 360448

commit v4 on v3

--- a/solution.py
+++ b/solution.py
@@ -16,7 +16,7 @@
 ROWS = 176
 WIDTH = 1024
 HALF = 2048
-SUBS = 4
+SUBS = 8
 PIECE = 512 // SUBS
 QSUBS = 4
 QPIECE = 1024 // QSUBS
@@ -153,17 +153,16 @@
         landed(part, xr.at[4 + i])
         send(part, part, xs.at[8 + i], xr.at[8 + i], xdown)
 
+    send_wkv(0)
     send_x(0)
+    send_wkv(1)
     unpack_w(2)
     unpack_w(3)
-    send_wkv(0)
     send_x(1)
     unpack_w(4)
     unpack_w(5)
-    send_wkv(1)
-    send_x(2)
-    send_x(3)
-    send(x_ref, xall.at[c, k], ps.at[0], pr.at[0], partner)
+    send_wkv(2)
+    send_wkv(3)
 
     def send_wq(s):
         for way, to in ((0, yup), (1, ydown)):
@@ -207,25 +206,34 @@
         if d < 3:
             send(bnd.at[zo(d)], bnd.at[zo(d)], bs.at[2 * d + 1], br.at[2 * d + 1], zdown)
 
+    send_x(2)
     forward_w(0)
-    send_wkv(2)
+    send_wkv(4)
+    forward_w(1)
+    send_wkv(5)
+    send_x(3)
     bounds_hop(0)
     relay_x(0)
     relay_x(1)
-    forward_w(1)
-    send_wkv(3)
+    send(x_ref, xall.at[c, k], ps.at[0], pr.at[0], partner)
+    forward_w(2)
+    send_wkv(6)
+    forward_w(3)
+    send_wkv(7)
     bounds_hop(1)
     for i in (2, 3):
         landed(xall.at[left, k, cuts[i], :], xr.at[i])
         landed(xall.at[right, k, cuts[3 - i], :], xr.at[7 - i])
     send(xall.at[left, k], xall.at[left, k], ps.at[1], pr.at[1], partner)
     send(xall.at[right, k], xall.at[right, k], ps.at[2], pr.at[2], partner)
-    forward_w(2)
+    forward_w(4)
     send_wq(0)
+    forward_w(5)
     bounds_hop(2)
     for i in range(4):
         landed(xall.at[far, k, cuts[i], :], xr.at[8 + i])
     send(xall.at[far, k], xall.at[far, k], ps.at[3], pr.at[3], partner)
+    forward_w(6)
     own_x.wait()
     own_g.wait()
     for i in (1, 2, 3):
@@ -246,9 +254,8 @@
                 xn[cc, at, s * 128 : (s + 1) * 128] = (v * inverse * gain).astype(BF16)
 
     normalise(k, pl.ds(pl.multiple_of(k * ROWS, ROWS), ROWS))
-    forward_w(3)
+    forward_w(7)
     send_wq(1)
-    bounds_hop(3)
     for n, block in enumerate((c, left, right, far)):
         landed(xall.at[block, 1 - k], pr.at[n])
     normalise(1 - k, pl.ds(pl.multiple_of((1 - k) * ROWS, ROWS), ROWS))
@@ -256,8 +263,9 @@
         out = slice(hh * 256, (hh + 1) * 256)
         acc[:, out] = jnp.dot(xn[2 * r], wkvo[hh, 0:1024], preferred_element_type=F32)
         acc[:, out] += jnp.dot(xn[2 * r + 1], wkvo[hh, 1024:2048], preferred_element_type=F32)
+    for hh in range(2):
+        out = slice(hh * 256, (hh + 1) * 256)
         acc[:, out] += jnp.dot(xn[2 * (1 - r) + zp], wkvx[zp, hh], preferred_element_type=F32)
-    bounds_hop(4)
     for s in range(SUBS):
         for way in range(2):
             landed(
@@ -282,7 +290,8 @@
     exchange = []
 
     def exchange_send(source, slot_of, ssems, rsems):
-        for hh in range(2):
+        for step in range(2):
+            hh = step
             yd = 2 * k + hh
             rel = lax.rem(y - yd + NY, NY)
             for j in range(2):
@@ -307,6 +316,14 @@
     send_wq(2)
     send_wq(3)
 
+    def ring_start(u):
+        block = kv_at(k, z, yo(u))
+        landed(block, akr.at[u])
+        send(block, block, rs.at[u], rp.at[u], zup)
+        send(block, block, rs.at[4 + u], rm.at[u], zdown)
+        send(block, block, pks.at[u], pkr.at[u], partner)
+
+    ring_start(0)
     accq[...] = jnp.dot(xn[2 * r], wqo[0:1024, :], preferred_element_type=F32)
     accq[...] += jnp.dot(xn[2 * r + 1], wqo[1024:2048, :], preferred_element_type=F32)
 
@@ -324,13 +341,6 @@
                 preferred_element_type=F32,
             )
 
-    project_q(0)
-    for u in ORDER:
-        block = kv_at(k, z, yo(u))
-        landed(block, akr.at[u])
-        send(block, block, rs.at[u], rp.at[u], zup)
-        send(block, block, rs.at[4 + u], rm.at[u], zdown)
-        send(block, block, pks.at[u], pkr.at[u], partner)
 
     def ring(d, pieces):
         up, down = zo(NZ - d), zo(d)
@@ -349,6 +359,13 @@
                     send(block, block, rs.at[d * 8 + 4 + u], rm.at[d * 4 + u], zdown)
                 n = (2 * d if d < 4 else 7) * 4 + u
                 send(block, block, pks.at[n], pkr.at[n], partner)
+    ring(1, (0,))
+    ring_start(1)
+    ring_start(3)
+    ring_start(2)
+    bounds_hop(3)
+    project_q(0)
+    ring(2, (0,))
     project_q(1)
     for hh in range(2):
         u = accq[:, hh * 128 : (hh + 1) * 128]
@@ -357,7 +374,8 @@
         stgq[hh, 1] = u[ROWS:].astype(BF16)
     exchange_send(stgq, lambda j: qb.at[y], aqs, aqr)
 
-    ring(1, ORDER)
+    ring(1, (1, 3, 2))
+    bounds_hop(4)
 
     mrun[...] = jnp.full_like(mrun, HIDE)
     oacc[...] = jnp.zeros_like(oacc)
@@ -371,7 +389,30 @@
     for n in range(4):
         qcat[n * ROWS : (n + 1) * ROWS, 0:128] = qb[n]
 
-    def attend(zz, diagonal):
+    def out_copy(yq):
+        return pltpu.make_async_remote_copy(
+            src_ref=osend.at[yq], dst_ref=obuf.at[y], send_sem=os_.at[yq],
+            recv_sem=orr.at[lax.rem(y - yq + NY, NY)],
+            device_id=dev(c, yq, z, k), device_id_type=MESH,
+        )
+
+    def out_tile(i):
+        rows = slice(i * 2 * ROWS, (i + 1) * 2 * ROWS)
+        result = (oacc[rows, 0:128] / oacc[rows, 128:256]).astype(BF16)
+        for n in range(2):
+            osend[2 * i + n] = result[n * ROWS : (n + 1) * ROWS]
+        for n in range(2):
+            yq = 2 * i + n
+
+            @pl.when(y == yq)
+            def _():
+                obuf[yq] = osend[yq]
+
+            @pl.when(y != yq)
+            def _():
+                out_copy(yq).start()
+
+    def attend(zz, diagonal, after=None):
         limit = bnd[zz]
         krow = lax.broadcasted_iota(jnp.int32, (8 * ROWS, 128), 0).astype(F32)
         kin = (krow >= limit[0:1, :]) & (krow < limit[1:2, :])
@@ -404,8 +445,10 @@
 
         first = scored(0)
         second = scored(1)
-        absorb(0, first)
-        absorb(1, second)
+        for i, scores in enumerate((first, second)):
+            absorb(i, scores)
+            if after is not None:
+                after(i)
 
     def shared(zz, n):
         for u in ORDER:
@@ -427,26 +470,33 @@
 
     shared(z, 0)
     attend(z, True)
-    ring(2, ORDER)
+    ring(3, (0,))
+    ring(2, (1,))
     attend_up(1)
+    ring(2, (3, 2))
     attend_down(1)
-    ring(3, ORDER[:2])
     attend_up(2)
-    ring(3, ORDER[2:])
+    ring(4, (0,))
+    ring(3, (1,))
     attend_down(2)
-    ring(4, ORDER)
+    ring(3, (3, 2))
     attend_up(3)
+    ring(4, (3,))
     attend_down(3)
-    attend_up(4)
-
-    result = (oacc[:, 0:128] / oacc[:, 128:256]).astype(BF16)
-    for n in range(4):
-        osend[n] = result[n * ROWS : (n + 1) * ROWS]
-    obuf[y] = osend[y]
+    ring(4, (1, 2))
+    shared(zo(4), 7)
+
+    @pl.when(z >= 4)
+    def _():
+        attend(zo(4), False, out_tile)
+
+    @pl.when(z < 4)
+    def _():
+        out_tile(0)
+        out_tile(1)
+
     for dy in (1, 2, 3):
-        send(osend.at[yo(dy)], obuf.at[y], os_.at[dy - 1], orr.at[NY - dy - 1], dev(c, yo(dy), z, k))
-    for dy in (1, 2, 3):
-        landed(obuf.at[yo(dy)], orr.at[dy - 1])
+        landed(obuf.at[yo(dy)], orr.at[dy])
     for h in range(4):
         o_ref[:, h * 128 : (h + 1) * 128] = obuf[h]
 
@@ -458,6 +508,12 @@
                 src_ref=move[0], dst_ref=move[1], send_sem=move[2], recv_sem=move[3],
                 device_id=to, device_id_type=MESH,
             ).wait_send()
+
+    for yq in range(NY):
+
+        @pl.when(y != yq)
+        def _():
+            out_copy(yq).wait_send()
 
     for copy in pending:
         copy.wait_send()
@@ -508,7 +564,7 @@
         dma((4,)), dma((4,)), dma((4,)), dma((4,)),
         dma((32,)), dma((16,)), dma((16,)),
         dma((32,)), dma((32,)),
-        dma((3,)), dma((3,)),
+        dma((4,)), dma((4,)),
     ]
     return pl.pallas_call(
         kernel,

time: 75.3 us -> 73.6 us (0.977)
  Pallas kernels: 73.5 us -> 71.9 us
    pallas_call x1, Pallas kernels: 73.5 us -> 71.9 us  [per_device(): pl.pallas_call(kernel, out_shape=jax.ShapeDtypeStruct((ROWS, 512), BF16),...]
where the time goes in v4:
time: 73.6 us; the launch traced here: 73.5 us
  Pallas kernels  71.9 us (98%)
  local copies, waits for them, and re-layouts  1.61 us (2%)
    pallas_call x1, Pallas kernels, per_device(): pl.pallas_call(kernel, out_shape=jax.ShapeDtypeStruct((ROWS, 512), BF16),...  71.9 us
    unnamed x1, local copies, waits for them, and re-layouts  1.61 us

profile of v4, /device:TPU:1, one launch (start us, length us, event | category | flops | bytes accessed | tf_op | source)
XLA Modules:
  0.0 73.5 jit_solution(15390790748803875936)
XLA Ops:
  0.0 71.9 %attention_block.1 = bf16[176,512]{1,0:T(8,128)(2,1)} custom-call(bf16[176,1024]{1,0:T(8,128)(2,1)} %x_ref.1, bf16[8,128]{1,0:T(8,128)(2,1)} %bitcast.2, bf16[2048,4,384]{2,1,0:T(4,128)(2,1)} %w_ref.1, s32[1,176]{1,0:T(1,128)} %bitcast.3, f32[1,128]{1,0:T(1,128)} %constant.2.clone.inv_ref), custom_call_target="tpu_custom_call" | custom-call | tf_op jit(solution)/shard_map/attention_block/pallas_call | solution.py:569
  71.9 1.6 %copy.7 = bf16[176,512]{1,0:T(8,128)(2,1)} copy(bf16[176,512]{1,0:T(8,128)(2,1)} %attention_block.1) | data formatting | bytes 360448

commit v5 on v4

--- a/solution.py
+++ b/solution.py
@@ -234,6 +234,8 @@
         landed(xall.at[far, k, cuts[i], :], xr.at[8 + i])
     send(xall.at[far, k], xall.at[far, k], ps.at[3], pr.at[3], partner)
     forward_w(6)
+    forward_w(7)
+    send_wq(1)
     own_x.wait()
     own_g.wait()
     for i in (1, 2, 3):
@@ -254,8 +256,6 @@
                 xn[cc, at, s * 128 : (s + 1) * 128] = (v * inverse * gain).astype(BF16)
 
     normalise(k, pl.ds(pl.multiple_of(k * ROWS, ROWS), ROWS))
-    forward_w(7)
-    send_wq(1)
     for n, block in enumerate((c, left, right, far)):
         landed(xall.at[block, 1 - k], pr.at[n])
     normalise(1 - k, pl.ds(pl.multiple_of((1 - k) * ROWS, ROWS), ROWS))
@@ -396,12 +396,19 @@
             device_id=dev(c, yq, z, k), device_id_type=MESH,
         )
 
+    def tile_rows(i):
+        if isinstance(i, int):
+            return slice(i * 2 * ROWS, (i + 1) * 2 * ROWS)
+        return pl.ds(pl.multiple_of(i * (2 * ROWS), 2 * ROWS), 2 * ROWS)
+
+    near = 1 - lax.rem(y, 2)
+
     def out_tile(i):
-        rows = slice(i * 2 * ROWS, (i + 1) * 2 * ROWS)
+        rows = tile_rows(i)
         result = (oacc[rows, 0:128] / oacc[rows, 128:256]).astype(BF16)
         for n in range(2):
             osend[2 * i + n] = result[n * ROWS : (n + 1) * ROWS]
-        for n in range(2):
+        for n in (near, 1 - near):
             yq = 2 * i + n
 
             @pl.when(y == yq)
@@ -412,7 +419,7 @@
             def _():
                 out_copy(yq).start()
 
-    def attend(zz, diagonal, after=None):
+    def attend(zz, diagonal, tiles=(0, 1), after=None):
         limit = bnd[zz]
         krow = lax.broadcasted_iota(jnp.int32, (8 * ROWS, 128), 0).astype(F32)
         kin = (krow >= limit[0:1, :]) & (krow < limit[1:2, :])
@@ -423,13 +430,13 @@
         values = jnp.concatenate([values, jnp.ones_like(values)], axis=1)
 
         def scored(i):
-            rows = slice(i * 2 * ROWS, (i + 1) * 2 * ROWS)
+            rows = tile_rows(i)
             return lax.dot_general(
                 qcat[rows, :], keys, (((1,), (1,)), ((), ())), preferred_element_type=F32
             )
 
         def absorb(i, scores):
-            rows = slice(i * 2 * ROWS, (i + 1) * 2 * ROWS)
+            rows = tile_rows(i)
             if diagonal:
                 shape = (2 * ROWS, 8 * ROWS)
                 qp = lax.broadcasted_iota(jnp.int32, shape, 0) + i * 4 * ROWS + 2 * ROWS * k
@@ -443,9 +450,9 @@
             oacc[rows, :] = oacc[rows, :] * jnp.concatenate([factor, factor], axis=1) + added
             mrun[rows, :] = newest
 
-        first = scored(0)
-        second = scored(1)
-        for i, scores in enumerate((first, second)):
+        first = scored(tiles[0])
+        second = scored(tiles[1])
+        for i, scores in zip(tiles, (first, second)):
             absorb(i, scores)
             if after is not None:
                 after(i)
@@ -488,12 +495,12 @@
 
     @pl.when(z >= 4)
     def _():
-        attend(zo(4), False, out_tile)
+        attend(zo(4), False, (1 - yh, yh), out_tile)
 
     @pl.when(z < 4)
     def _():
-        out_tile(0)
-        out_tile(1)
+        out_tile(1 - yh)
+        out_tile(yh)
 
     for dy in (1, 2, 3):
         landed(obuf.at[yo(dy)], orr.at[dy])

time: 73.6 us -> 73.3 us (level)
  no operation moved by 1% of the time
where the time goes in v5:
time: 73.3 us; the launch traced here: 73.1 us
  Pallas kernels  71.5 us (98%)
  local copies, waits for them, and re-layouts  1.61 us (2%)
    pallas_call x1, Pallas kernels, per_device(): pl.pallas_call(kernel, out_shape=jax.ShapeDtypeStruct((ROWS, 512), BF16),...  71.5 us
    unnamed x1, local copies, waits for them, and re-layouts  1.61 us

profile of v5, /device:TPU:1, one launch (start us, length us, event | category | flops | bytes accessed | tf_op | source)
XLA Modules:
  0.0 73.1 jit_solution(7635583823176926709)
XLA Ops:
  0.0 71.5 %attention_block.1 = bf16[176,512]{1,0:T(8,128)(2,1)} custom-call(bf16[176,1024]{1,0:T(8,128)(2,1)} %x_ref.1, bf16[8,128]{1,0:T(8,128)(2,1)} %bitcast.2, bf16[2048,4,384]{2,1,0:T(4,128)(2,1)} %w_ref.1, s32[1,176]{1,0:T(1,128)} %bitcast.3, f32[1,128]{1,0:T(1,128)} %constant.2.clone.inv_ref), custom_call_target="tpu_custom_call" | custom-call | tf_op jit(solution)/shard_map/attention_block/pallas_call | solution.py:576
  71.5 1.6 %copy.7 = bf16[176,512]{1,0:T(8,128)(2,1)} copy(bf16[176,512]{1,0:T(8,128)(2,1)} %attention_block.1) | data formatting | bytes 360448
